TPU v7x, 32 devices: a whole 2x2x4 slice. The times are simulated.
32 devices in a mesh: seq: 16 (over z, y, x), mp: 2 (over core).
Axes of the slice: x: 2, y: 2, z: 4, core: 2. Of those that a mesh axis runs over, the one named last changes fastest.
Arguments:
- inner_act: bfloat16 [2048, 6144], P('seq', 'mp'), may hold values from -6 to 6
- gate_act: bfloat16 [2048, 6144], P('seq', 'mp'), may hold values from -6 to 6
- x_proj: bfloat16 [6144, 224], P('mp'), may hold values from -0.078125 to 0.078125
- dt_proj: bfloat16 [192, 6144], P(None, 'mp'), may hold values from -0.4375 to 0.4375
- dt_bias: float32 [6144], P('mp'), may hold values from -5.5 to -3.5
- a_log: float32 [16, 6144], P(None, 'mp'), may hold values from -12 to 2.3
- skip: float32 [6144], P('mp'), may hold values from 0.5 to 1.5
Outputs:
- mixed_out: bfloat16 [2048, 6144], P('seq', 'mp')
All inputs are finite; a program needn't handle non-finite values.
Results may differ from a plain program's by a relative error of at most 0.0095.
Values sent between devices are 32-bit elements; how exact they have to be, the bound alone decides.
A program may use at most 128 MiB of HBM per device.

v0:
```python
import functools
import math

import jax
import jax.numpy as jnp
from jax import lax
from jax.experimental import pallas as pl
from jax.experimental.pallas import tpu as pltpu
from jax.sharding import PartitionSpec as P

LANES = 128
SUB = 8
TILE = LANES * SUB
UNROLL = 8
LOG2E = 1.4426950408889634
F32 = jnp.float32


def softplus(x):
    return jnp.maximum(x, 0.0) + jnp.log1p(jnp.exp(-jnp.abs(x)))


def kernel(seq, mp, tokens, inner, rank, states,
           u_ref, g_ref, xp_ref, dtp_ref, bias_ref, alog_ref, skip_ref, out_ref,
           proj, bs, cs, rate, dts, drv, ys, tot, got, pre, hand, ent,
           mp_send, mp_recv, tot_send, tot_recv, hand_send, hand_recv):
    blocks = pl.cdiv(inner, TILE)
    digit = 4
    stride = seq // digit
    bits = int(math.log2(stride))
    me = lax.axis_index("seq")
    my_mp = lax.axis_index("mp")
    plane = me // stride
    above = lax.rem(me + stride, seq)
    below = lax.rem(me + seq - stride, seq)

    def partner(r):
        bit = lax.rem(me // (1 << r), 2)
        return me + (1 - 2 * bit) * (1 << r), bit

    barrier = pltpu.get_barrier_semaphore()
    for m in range(1, mp):
        pl.semaphore_signal(barrier, inc=1, device_id={"mp": lax.rem(my_mp + m, mp)},
                            device_id_type=pl.DeviceIdType.MESH)
    for r in range(bits):
        pl.semaphore_signal(barrier, inc=1, device_id={"seq": partner(r)[0]},
                            device_id_type=pl.DeviceIdType.MESH)
    for other in (above, below):
        pl.semaphore_signal(barrier, inc=1, device_id={"seq": other},
                            device_id_type=pl.DeviceIdType.MESH)

    proj[my_mp] = jnp.dot(u_ref[...], xp_ref[...], preferred_element_type=F32)
    pl.semaphore_wait(barrier, (mp - 1) + bits + 2)
    shares = []
    for m in range(1, mp):
        copy = pltpu.make_async_remote_copy(
            src_ref=proj.at[my_mp], dst_ref=proj.at[my_mp],
            send_sem=mp_send.at[m - 1], recv_sem=mp_recv.at[m - 1],
            device_id={"mp": lax.rem(my_mp + m, mp)},
            device_id_type=pl.DeviceIdType.MESH)
        copy.start()
        shares.append(copy)

    for k in range(blocks):
        for j in range(min(SUB, inner // LANES - k * SUB)):
            lo = (k * SUB + j) * LANES
            rate[k, pl.ds(j, states, stride=SUB), :] = (
                jnp.exp(alog_ref[:, lo:lo + LANES]) * (-LOG2E))

    for copy in shares:
        copy.wait()
    whole = proj[0]
    for m in range(1, mp):
        whole = whole + proj[m]
    low = whole[:, :rank].astype(jnp.bfloat16)
    for n in range(states):
        bs[n] = jnp.broadcast_to(whole[:, rank + n:rank + n + 1], (tokens, LANES))
        cs[n] = jnp.broadcast_to(
            whole[:, rank + states + n:rank + states + n + 1], (tokens, LANES))

    def lanes_of(k):
        return min(SUB, inner // LANES - k * SUB)

    def steps(k):
        @pl.loop(0, lanes_of(k))
        def _(j):
            lo = pl.multiple_of((k * SUB + j) * LANES, LANES)
            cols = pl.ds(lo, LANES)
            dt = softplus(jnp.dot(low, dtp_ref[:, cols], preferred_element_type=F32)
                          + bias_ref[:, cols])
            dts[k, pl.ds(j, tokens, stride=SUB), :] = dt
            drv[k, pl.ds(j, tokens, stride=SUB), :] = dt * u_ref[:, cols].astype(F32)

    def tile(ref, k, i):
        return ref[k, pl.ds(pl.multiple_of(i * SUB, SUB), SUB), :]

    def scan(k):
        rates = [rate[k, n * SUB:(n + 1) * SUB, :] for n in range(states)]

        def body(it, carry):
            total, hs = carry[0], list(carry[1:])
            for i in range(UNROLL):
                t = it * UNROLL + i
                dt = tile(dts, k, t)
                dr = tile(drv, k, t)
                total = total + dt
                acc = [None, None]
                for n in range(states):
                    b = bs[n, pl.ds(t, 1), :]
                    c = cs[n, pl.ds(t, 1), :]
                    hs[n] = jnp.exp2(rates[n] * dt) * hs[n] + b * dr
                    term = c * hs[n]
                    acc[n % 2] = term if acc[n % 2] is None else acc[n % 2] + term
                ys[k, pl.ds(pl.multiple_of(t * SUB, SUB), SUB), :] = acc[0] + acc[1]
            return (total, *hs)

        zero = jnp.zeros((SUB, LANES), F32)
        final = lax.fori_loop(0, tokens // UNROLL, body, (zero,) * (states + 1))
        for n in range(states):
            tot[0, k, n] = final[1 + n]
            pre[k, n] = zero
        tot[0, k, states] = final[0]
        pre[k, states] = zero

    def exchange(r, k):
        return pltpu.make_async_remote_copy(
            src_ref=tot.at[r, k], dst_ref=got.at[r, k],
            send_sem=tot_send.at[r, k], recv_sem=tot_recv.at[r, k],
            device_id={"seq": partner(r)[0]}, device_id_type=pl.DeviceIdType.MESH)

    def join(r, k):
        bit = partner(r)[1]
        exchange(r, k).wait_recv()
        mine_s = tot[r, k, states]
        theirs_s = got[r, k, states]

        @pl.when(bit == 1)
        def _():
            pre_s = pre[k, states]
            for n in range(states):
                rt = rate[k, n * SUB:(n + 1) * SUB, :]
                theirs = got[r, k, n]
                tot[r + 1, k, n] = jnp.exp2(rt * mine_s) * theirs + tot[r, k, n]
                pre[k, n] = jnp.exp2(rt * pre_s) * theirs + pre[k, n]
            pre[k, states] = pre_s + theirs_s

        @pl.when(bit == 0)
        def _():
            for n in range(states):
                rt = rate[k, n * SUB:(n + 1) * SUB, :]
                tot[r + 1, k, n] = jnp.exp2(rt * theirs_s) * tot[r, k, n] + got[r, k, n]

        tot[r + 1, k, states] = mine_s + theirs_s

    def pass_on(k):
        return pltpu.make_async_remote_copy(
            src_ref=hand.at[0, k], dst_ref=hand.at[1, k],
            send_sem=hand_send.at[k], recv_sem=hand_recv.at[k],
            device_id={"seq": above}, device_id_type=pl.DeviceIdType.MESH)

    def forward(k):
        @pl.when(plane == 0)
        def _():
            for n in range(states):
                hand[0, k, n] = tot[bits, k, n]
                ent[k, n] = pre[k, n]
            pass_on(k).start()

        @pl.when(jnp.logical_and(plane > 0, plane < digit - 1))
        def _():
            pass_on(k).wait_recv()
            all_s = tot[bits, k, states]
            for n in range(states):
                rt = rate[k, n * SUB:(n + 1) * SUB, :]
                hand[0, k, n] = jnp.exp2(rt * all_s) * hand[1, k, n] + tot[bits, k, n]
            pass_on(k).start()

    def enter(k):
        @pl.when(plane == digit - 1)
        def _():
            pass_on(k).wait_recv()

        @pl.when(plane > 0)
        def _():
            pre_s = pre[k, states]
            for n in range(states):
                rt = rate[k, n * SUB:(n + 1) * SUB, :]
                ent[k, n] = jnp.exp2(rt * pre_s) * hand[1, k, n] + pre[k, n]

    def correct(k):
        rates = [rate[k, n * SUB:(n + 1) * SUB, :] for n in range(states)]
        ents = [ent[k, n] for n in range(states)]

        def body(it, total):
            for i in range(UNROLL):
                t = it * UNROLL + i
                total = total + tile(dts, k, t)
                acc = [tile(ys, k, t), None]
                for n in range(states):
                    c = cs[n, pl.ds(t, 1), :]
                    term = c * (jnp.exp2(rates[n] * total) * ents[n])
                    acc[n % 2] = term if acc[n % 2] is None else acc[n % 2] + term
                ys[k, pl.ds(pl.multiple_of(t * SUB, SUB), SUB), :] = acc[0] + acc[1]
            return total

        lax.fori_loop(0, tokens // UNROLL, body, jnp.zeros((SUB, LANES), F32))

    def finish(k):
        @pl.loop(0, lanes_of(k))
        def _(j):
            lo = pl.multiple_of((k * SUB + j) * LANES, LANES)
            cols = pl.ds(lo, LANES)
            y = ys[k, pl.ds(j, tokens, stride=SUB), :]
            g = g_ref[:, cols].astype(F32)
            mixed = (y + skip_ref[:, cols] * u_ref[:, cols].astype(F32)) * (
                g / (1.0 + jnp.exp(-g)))
            out_ref[:, cols] = mixed.astype(out_ref.dtype)

    for step in range(blocks + bits):
        if step < blocks:
            steps(step)
            scan(step)
            exchange(0, step).start()
        for r in range(bits):
            k = step - 1 - r
            if 0 <= k < blocks:
                join(r, k)
                if r + 1 < bits:
                    exchange(r + 1, k).start()
                else:
                    forward(k)
    for k in range(blocks):
        enter(k)
        correct(k)
        finish(k)
    for k in range(blocks):
        for r in range(bits):
            exchange(r, k).wait_send()

        @pl.when(plane < digit - 1)
        def _():
            pass_on(k).wait_send()


def solution(mesh):
    seq, mp = mesh.shape["seq"], mesh.shape["mp"]

    def per_device(inner_act, gate_act, x_proj, dt_proj, dt_bias, a_log, skip):
        tokens, inner = inner_act.shape
        rank, states = dt_proj.shape[0], a_log.shape[0]
        blocks = pl.cdiv(inner, TILE)
        bits = int(math.log2(seq // 4))
        vmem = pl.BlockSpec(memory_space=pltpu.VMEM)
        msg = (states + 1, SUB, LANES)
        return pl.pallas_call(
            functools.partial(kernel, seq, mp, tokens, inner, rank, states),
            out_shape=jax.ShapeDtypeStruct((tokens, inner), jnp.bfloat16),
            in_specs=[vmem] * 7,
            out_specs=vmem,
            scratch_shapes=[
                pltpu.VMEM((mp, tokens, x_proj.shape[1]), F32),
                pltpu.VMEM((states, tokens, LANES), F32),
                pltpu.VMEM((states, tokens, LANES), F32),
                pltpu.VMEM((blocks, states * SUB, LANES), F32),
                pltpu.VMEM((blocks, tokens * SUB, LANES), F32),
                pltpu.VMEM((blocks, tokens * SUB, LANES), F32),
                pltpu.VMEM((blocks, tokens * SUB, LANES), F32),
                pltpu.VMEM((bits + 1, blocks) + msg, F32),
                pltpu.VMEM((bits, blocks) + msg, F32),
                pltpu.VMEM((blocks,) + msg, F32),
                pltpu.VMEM((2, blocks, states, SUB, LANES), F32),
                pltpu.VMEM((blocks, states, SUB, LANES), F32),
                pltpu.SemaphoreType.DMA((mp - 1,)),
                pltpu.SemaphoreType.DMA((mp - 1,)),
                pltpu.SemaphoreType.DMA((bits, blocks)),
                pltpu.SemaphoreType.DMA((bits, blocks)),
                pltpu.SemaphoreType.DMA((blocks,)),
                pltpu.SemaphoreType.DMA((blocks,)),
            ],
            compiler_params=pltpu.CompilerParams(
                collective_id=0, has_side_effects=True,
                vmem_limit_bytes=48 * 1024 * 1024),
        )(inner_act, gate_act, x_proj, dt_proj, dt_bias.reshape(1, inner), a_log,
          skip.reshape(1, inner))

    placed = (
        P("seq", "mp"),
        P("seq", "mp"),
        P("mp", None),
        P(None, "mp"),
        P("mp"),
        P(None, "mp"),
        P("mp"),
    )
    return jax.shard_map(
        per_device, mesh=mesh, in_specs=placed, out_specs=P("seq", "mp"), check_vma=False
    )
```

profile of v0, /device:TPU:16, one launch (start us, length us, event | category | flops | bytes accessed | tf_op | source)
XLA Modules:
  0.0 42.3 jit_solution(12471253139837940748)
XLA Ops:
  0.0 0.0 copy-start
  0.0 0.0 copy-start.1
  0.0 0.0 copy-start.4
  0.0 1.8 %copy.8.xp_ref = bf16[3072,224]{1,0:T(8,128)(2,1)S(1)} copy(bf16[3072,224]{0,1:T(8,128)(2,1)} %param.9) | data formatting | bytes 2752512 | tf_op args[2]
  1.8 0.0 copy-done
  1.8 0.1 copy-done.1
  1.9 0.0 copy-done.4
  1.9 0.0 copy-start.2
  1.9 1.1 %copy-done.2 = bf16[128,3072]{1,0:T(8,128)(2,1)S(1)} copy-done((bf16[128,3072]{1,0:T(8,128)(2,1)S(1)}, bf16[128,3072]{1,0:T(8,128)(2,1)}, u32[]{:S(2)}) %copy-start.2) | copy-done | bytes 786456
  3.0 0.0 copy-start.3
  3.0 0.9 %copy-done.3 = f32[16,3072]{1,0:T(8,128)S(1)} copy-done((f32[16,3072]{1,0:T(8,128)S(1)}, f32[16,3072]{1,0:T(8,128)}, u32[]{:S(2)}) %copy-start.3) | copy-done | bytes 196632
  4.0 0.0 copy-start.5
  4.0 0.7 %copy-done.5 = f32[3072]{0:T(1024)S(1)} copy-done((f32[3072]{0:T(1024)S(1)}, f32[3072]{0:T(1024)}, u32[]{:S(2)}) %copy-start.5) | copy-done | bytes 12312
  4.7 36.7 %shard_map.73 = bf16[128,3072]{1,0:T(8,128)(2,1)S(1)} custom-call(bf16[128,3072]{1,0:T(8,128)(2,1)S(1)} %copy-done.1, bf16[128,3072]{1,0:T(8,128)(2,1)S(1)} %copy-done.2, bf16[3072,224]{1,0:T(8,128)(2,1)S(1)} %copy.8.xp_ref, bf16[192,3072]{1,0:T(8,128)(2,1)S(1)} %copy-done, f32[1,3072]{1,0:T(1,128)S(1)} %bitcast.2, f32[16,3072]{1,0:T(8,128)S(1)} %copy-done.3, ...), custom_call_target="tpu_custom_call" | custom-call | tf_op jit(solution)/shard_map/pallas_call | solution.py:255
  41.4 0.9 %copy.10 = bf16[128,3072]{1,0:T(8,128)(2,1)} copy(bf16[128,3072]{1,0:T(8,128)(2,1)S(1)} %shard_map.73) | data formatting | bytes 1572864
Async XLA Ops:
  0.0 1.8 %copy-start = (bf16[192,3072]{1,0:T(8,128)(2,1)S(1)}, bf16[192,3072]{1,0:T(8,128)(2,1)}, u32[]{:S(2)}) copy-start(bf16[192,3072]{1,0:T(8,128)(2,1)} %dtp_ref.1) | copy-start | bytes 3538948
  0.0 1.9 %copy-start.1 = (bf16[128,3072]{1,0:T(8,128)(2,1)S(1)}, bf16[128,3072]{1,0:T(8,128)(2,1)}, u32[]{:S(2)}) copy-start(bf16[128,3072]{1,0:T(8,128)(2,1)} %u_ref.1) | copy-start | bytes 2359300
  0.0 1.9 %copy-start.4 = (f32[3072]{0:T(1024)S(1)}, f32[3072]{0:T(1024)}, u32[]{:S(2)}) copy-start(f32[3072]{0:T(1024)} %param.11) | copy-start | bytes 36868
  1.9 1.1 %copy-start.2 = (bf16[128,3072]{1,0:T(8,128)(2,1)S(1)}, bf16[128,3072]{1,0:T(8,128)(2,1)}, u32[]{:S(2)}) copy-start(bf16[128,3072]{1,0:T(8,128)(2,1)} %g_ref.1) | copy-start | bytes 2359300
  3.0 0.9 %copy-start.3 = (f32[16,3072]{1,0:T(8,128)S(1)}, f32[16,3072]{1,0:T(8,128)}, u32[]{:S(2)}) copy-start(f32[16,3072]{1,0:T(8,128)} %alog_ref.1) | copy-start | bytes 589828
  4.0 0.7 %copy-start.5 = (f32[3072]{0:T(1024)S(1)}, f32[3072]{0:T(1024)}, u32[]{:S(2)}) copy-start(f32[3072]{0:T(1024)} %param.13) | copy-start | bytes 36868
where the time goes:
time: 42.5 us; the launch traced here: 42.3 us
  Pallas kernels  36.7 us (86%)
  local copies, waits for them, and re-layouts  5.53 us (13%)
    pallas_call x1, Pallas kernels, per_device(): pl.pallas_call(functools.partial(kernel, seq, mp, tokens, inner, rank, st...  36.7 us
    unnamed x14, local copies, waits for them, and re-layouts  5.53 us

commit v1 on v0

v1 whole, which is shorter than its diff:
```python
import functools

import jax
import jax.numpy as jnp
from jax import lax
from jax.experimental import pallas as pl
from jax.experimental.pallas import tpu as pltpu
from jax.sharding import PartitionSpec as P

LANES = 128
SUB = 8
TILE = LANES * SUB
UNROLL = 8
LOG2E = 1.4426950408889634
F32 = jnp.float32


def softplus(x):
    e = jnp.exp(-jnp.abs(x))
    series = e * (1.0 - e * (0.5 - e * (1.0 / 3.0 - e * (0.25 - e * 0.2))))
    return jnp.maximum(x, 0.0) + jnp.where(e < 0.03125, series, jnp.log(1.0 + e))


def kernel(seq, mp, tokens, inner, rank, states,
           u_hbm, g_hbm, xp_hbm, dtp_hbm, bias_hbm, alog_hbm, skip_hbm, out_ref,
           u_ref, g_ref, xp_ref, dtp_ref, bias_ref, alog_ref, skip_ref,
           proj, bs, cs, rate, raw, dts, drv, ys, tot, sums, got_e, got_s, back, ent, far, near,
           in_sem, mp_send, mp_recv, e_send, e_recv, s_send, s_recv, b_send, b_recv,
           f_send, f_recv):
    blocks = pl.cdiv(inner, TILE)
    group = states
    groups = seq // group
    me = lax.axis_index("seq")
    my_mp = lax.axis_index("mp")
    mine = lax.rem(me, group)
    my_group = me // group
    base = my_group * group

    loads = [pltpu.make_async_copy(src, dst, in_sem.at[i]) for i, (src, dst) in enumerate((
        (u_hbm, u_ref), (xp_hbm, xp_ref), (alog_hbm, alog_ref), (dtp_hbm, dtp_ref),
        (bias_hbm, bias_ref), (g_hbm, g_ref), (skip_hbm, skip_ref)))]
    for load in loads:
        load.start()

    barrier = pltpu.get_barrier_semaphore()
    for m in range(1, mp):
        pl.semaphore_signal(barrier, inc=1, device_id={"mp": lax.rem(my_mp + m, mp)},
                            device_id_type=pl.DeviceIdType.MESH)
    for p in range(1, group):
        pl.semaphore_signal(barrier, inc=1,
                            device_id={"seq": base + lax.rem(mine + p, group)},
                            device_id_type=pl.DeviceIdType.MESH)
    for p in range(1, groups):
        pl.semaphore_signal(barrier, inc=1, device_id={"seq": lax.rem(me + p * group, seq)},
                            device_id_type=pl.DeviceIdType.MESH)

    loads[0].wait()
    loads[1].wait()
    proj[my_mp] = lax.dot_general(u_ref[...], xp_ref[...], (((1,), (1,)), ((), ())),
                                  preferred_element_type=F32)
    pl.semaphore_wait(barrier, (mp - 1) + (group - 1) + (groups - 1))
    shares = []
    for m in range(1, mp):
        copy = pltpu.make_async_remote_copy(
            src_ref=proj.at[my_mp], dst_ref=proj.at[my_mp],
            send_sem=mp_send.at[m - 1], recv_sem=mp_recv.at[m - 1],
            device_id={"mp": lax.rem(my_mp + m, mp)},
            device_id_type=pl.DeviceIdType.MESH)
        copy.start()
        shares.append(copy)

    loads[2].wait()
    for k in range(blocks):
        for j in range(min(SUB, inner // LANES - k * SUB)):
            lo = (k * SUB + j) * LANES
            rate[k, pl.ds(j, states, stride=SUB), :] = (
                jnp.exp(alog_ref[:, lo:lo + LANES]) * (-LOG2E))
    loads[3].wait()
    loads[4].wait()

    for copy in shares:
        copy.wait()
    whole = proj[0]
    for m in range(1, mp):
        whole = whole + proj[m]
    low = whole[:, :rank].astype(jnp.bfloat16)

    def lanes_of(k):
        return min(SUB, inner // LANES - k * SUB)

    def tile(ref, k, i):
        return ref[k, pl.ds(pl.multiple_of(i * SUB, SUB), SUB), :]

    def steps(k):
        width = lanes_of(k) * LANES
        raw[:, :width] = jnp.dot(low, dtp_ref[:, k * TILE:k * TILE + width],
                                 preferred_element_type=F32)
        @pl.loop(0, lanes_of(k))
        def _(j):
            lo = pl.multiple_of((k * SUB + j) * LANES, LANES)
            cols = pl.ds(lo, LANES)
            dt = softplus(raw[:, pl.ds(pl.multiple_of(j * LANES, LANES), LANES)]
                          + bias_ref[:, cols])
            dts[k, pl.ds(j, tokens, stride=SUB), :] = dt
            drv[k, pl.ds(j, tokens, stride=SUB), :] = dt * u_ref[:, cols].astype(F32)
            sums[k, pl.ds(j, 1), :] = jnp.sum(dt, axis=0, keepdims=True)

        got_s[k, 0] = sums[k]

        @pl.loop(1, group)
        def _(p):
            pltpu.make_async_remote_copy(
                src_ref=sums.at[k], dst_ref=got_s.at[k, group - p],
                send_sem=s_send.at[k], recv_sem=s_recv.at[k],
                device_id={"seq": base + lax.rem(mine + p, group)},
                device_id_type=pl.DeviceIdType.MESH).start()

    def scan(k):
        rates = [rate[k, n * SUB:(n + 1) * SUB, :] for n in range(states)]

        def body(it, hs):
            hs = list(hs)
            for i in range(UNROLL):
                t = it * UNROLL + i
                dt = tile(dts, k, t)
                dr = tile(drv, k, t)
                acc = [None, None]
                for n in range(states):
                    b = bs[n, pl.ds(t, 1), :]
                    c = cs[n, pl.ds(t, 1), :]
                    hs[n] = jnp.exp2(rates[n] * dt) * hs[n] + b * dr
                    term = c * hs[n]
                    acc[n % 2] = term if acc[n % 2] is None else acc[n % 2] + term
                ys[k, pl.ds(pl.multiple_of(t * SUB, SUB), SUB), :] = acc[0] + acc[1]
            return tuple(hs)

        zero = jnp.zeros((SUB, LANES), F32)
        final = lax.fori_loop(0, tokens // UNROLL, body, (zero,) * states)
        for n in range(states):
            tot[k, n] = final[n]
        got_e[k, 0] = tot[k, mine]

        @pl.loop(1, group)
        def _(p):
            owner = lax.rem(mine + p, group)
            pltpu.make_async_remote_copy(
                src_ref=tot.at[k, owner], dst_ref=got_e.at[k, group - p],
                send_sem=e_send.at[k], recv_sem=e_recv.at[k],
                device_id={"seq": base + owner},
                device_id_type=pl.DeviceIdType.MESH).start()

    def drain(ref, k, sem):
        part = ref.at[k, pl.ds(1, group - 1)]
        pltpu.make_async_copy(part, part, sem.at[k]).wait()

    def own(k):
        drain(got_s, k, s_recv)
        drain(got_e, k, e_recv)
        rt = rate[k, pl.ds(pl.multiple_of(mine * SUB, SUB), SUB), :]
        slots = [lax.rem(j - mine + group, group) for j in range(group)]
        carry = jnp.zeros((SUB, LANES), F32)
        if groups > 1:
            end, span = carry, carry
            for slot in slots:
                end = jnp.exp2(rt * got_s[k, slot]) * end + got_e[k, slot]
                span = span + got_s[k, slot]
            near[k, 0] = end
            near[k, 1] = span
            sent = [pltpu.make_async_remote_copy(
                src_ref=near.at[k], dst_ref=far.at[k, groups - p],
                send_sem=f_send.at[k, p], recv_sem=f_recv.at[k, groups - p],
                device_id={"seq": lax.rem(me + p * group, seq)},
                device_id_type=pl.DeviceIdType.MESH) for p in range(1, groups)]
            for copy in sent:
                copy.start()
            for copy in sent:
                copy.wait()
            far[k, 0] = near[k]
            for g in range(groups - 1):
                slot = lax.rem(g - my_group + groups, groups)
                carry = jnp.where(
                    g < my_group, jnp.exp2(rt * far[k, slot, 1]) * carry + far[k, slot, 0], carry)
        for slot in slots:
            back[k, slot] = carry
            carry = jnp.exp2(rt * got_s[k, slot]) * carry + got_e[k, slot]
        ent[k, 0] = back[k, 0]

        @pl.loop(1, group)
        def _(p):
            pltpu.make_async_remote_copy(
                src_ref=back.at[k, p], dst_ref=ent.at[k, group - p],
                send_sem=b_send.at[k], recv_sem=b_recv.at[k],
                device_id={"seq": base + lax.rem(mine + p, group)},
                device_id_type=pl.DeviceIdType.MESH).start()

    def correct(k):
        drain(ent, k, b_recv)
        rates = [rate[k, n * SUB:(n + 1) * SUB, :] for n in range(states)]
        ents = [ent[k, lax.rem(n - mine + group, group)] for n in range(states)]

        def body(it, total):
            for i in range(UNROLL):
                t = it * UNROLL + i
                total = total + tile(dts, k, t)
                acc = [tile(ys, k, t), None]
                for n in range(states):
                    c = cs[n, pl.ds(t, 1), :]
                    term = c * (jnp.exp2(rates[n] * total) * ents[n])
                    acc[n % 2] = term if acc[n % 2] is None else acc[n % 2] + term
                ys[k, pl.ds(pl.multiple_of(t * SUB, SUB), SUB), :] = acc[0] + acc[1]
            return total

        lax.fori_loop(0, tokens // UNROLL, body, jnp.zeros((SUB, LANES), F32))

    def finish(k):
        @pl.loop(0, lanes_of(k))
        def _(j):
            lo = pl.multiple_of((k * SUB + j) * LANES, LANES)
            cols = pl.ds(lo, LANES)
            y = ys[k, pl.ds(j, tokens, stride=SUB), :]
            g = g_ref[:, cols].astype(F32)
            mixed = (y + skip_ref[:, cols] * u_ref[:, cols].astype(F32)) * (
                g / (1.0 + jnp.exp(-g)))
            out_ref[:, cols] = mixed.astype(out_ref.dtype)

    if inner % TILE:
        sums[blocks - 1] = jnp.zeros((SUB, LANES), F32)
    for k in range(blocks):
        steps(k)
    for n in range(states):
        bs[n] = jnp.broadcast_to(whole[:, rank + n:rank + n + 1], (tokens, LANES))
        cs[n] = jnp.broadcast_to(
            whole[:, rank + states + n:rank + states + n + 1], (tokens, LANES))
    for k in range(blocks):
        scan(k)
        if k > 0:
            own(k - 1)
    loads[5].wait()
    loads[6].wait()
    for k in range(blocks - 1):
        correct(k)
        finish(k)
        if k == 0:
            own(blocks - 1)
    if blocks == 1:
        own(0)
    correct(blocks - 1)
    finish(blocks - 1)
    for k in range(blocks):
        drain(got_s, k, s_send)
        drain(got_e, k, e_send)
        drain(back, k, b_send)


def solution(mesh):
    seq, mp = mesh.shape["seq"], mesh.shape["mp"]

    def per_device(inner_act, gate_act, x_proj, dt_proj, dt_bias, a_log, skip):
        tokens, inner = inner_act.shape
        rank, states = dt_proj.shape[0], a_log.shape[0]
        blocks = pl.cdiv(inner, TILE)
        group, groups = states, seq // states
        hbm = pl.BlockSpec(memory_space=pltpu.MemorySpace.HBM)
        args = (inner_act, gate_act, x_proj.T, dt_proj, dt_bias.reshape(1, inner), a_log,
                skip.reshape(1, inner))
        cell = (SUB, LANES)
        dma = pltpu.SemaphoreType.DMA
        return pl.pallas_call(
            functools.partial(kernel, seq, mp, tokens, inner, rank, states),
            out_shape=jax.ShapeDtypeStruct((tokens, inner), jnp.bfloat16),
            in_specs=[hbm] * len(args),
            out_specs=pl.BlockSpec(memory_space=pltpu.VMEM),
            scratch_shapes=[pltpu.VMEM(a.shape, a.dtype) for a in args] + [
                pltpu.VMEM((mp, tokens, x_proj.shape[1]), F32),
                pltpu.VMEM((states, tokens, LANES), F32),
                pltpu.VMEM((states, tokens, LANES), F32),
                pltpu.VMEM((blocks, states * SUB, LANES), F32),
                pltpu.VMEM((tokens, TILE), F32),
                pltpu.VMEM((blocks, tokens * SUB, LANES), F32),
                pltpu.VMEM((blocks, tokens * SUB, LANES), F32),
                pltpu.VMEM((blocks, tokens * SUB, LANES), F32),
                pltpu.VMEM((blocks, states) + cell, F32),
                pltpu.VMEM((blocks,) + cell, F32),
                pltpu.VMEM((blocks, group) + cell, F32),
                pltpu.VMEM((blocks, group) + cell, F32),
                pltpu.VMEM((blocks, group) + cell, F32),
                pltpu.VMEM((blocks, group) + cell, F32),
                pltpu.VMEM((blocks, groups, 2) + cell, F32),
                pltpu.VMEM((blocks, 2) + cell, F32),
                dma((len(args),)),
                dma((mp - 1,)), dma((mp - 1,)),
                dma((blocks,)), dma((blocks,)),
                dma((blocks,)), dma((blocks,)),
                dma((blocks,)), dma((blocks,)),
                dma((blocks, groups)), dma((blocks, groups)),
            ],
            compiler_params=pltpu.CompilerParams(
                collective_id=0, has_side_effects=True,
                vmem_limit_bytes=48 * 1024 * 1024),
        )(*args)

    placed = (
        P("seq", "mp"),
        P("seq", "mp"),
        P("mp", None),
        P(None, "mp"),
        P("mp"),
        P(None, "mp"),
        P("mp"),
    )
    return jax.shard_map(
        per_device, mesh=mesh, in_specs=placed, out_specs=P("seq", "mp"), check_vma=False
    )
```

time: 42.5 us -> 40.9 us (0.962)
  the two profiles are of different devices: /device:TPU:16 before, /device:TPU:0 now
where the time goes in v1:
time: 40.9 us; the launch traced here: 40.5 us
  Pallas kernels  32.4 us (79%)
  local copies, waits for them, and re-layouts  8.09 us (20%)
    pallas_call x1, Pallas kernels, per_device(): pl.pallas_call(functools.partial(kernel, seq, mp, tokens, inner, rank, st...  32.4 us
    unnamed x15, local copies, waits for them, and re-layouts  8.09 us

profile of v1, /device:TPU:0, one launch (start us, length us, event | category | flops | bytes accessed | tf_op | source)
XLA Modules:
  0.0 40.5 jit_solution(6134954575840772109)
XLA Ops:
  0.0 0.0 copy-start
  0.0 1.3 %copy-done = bf16[3072,224]{0,1:T(8,128)(2,1)S(1)} copy-done((bf16[3072,224]{0,1:T(8,128)(2,1)S(1)}, bf16[3072,224]{0,1:T(8,128)(2,1)}, u32[]{:S(2)}) %copy-start) | copy-done | bytes 1376280
  1.3 0.0 copy-start.1
  1.3 1.3 %copy-done.1 = bf16[192,3072]{1,0:T(8,128)(2,1)S(1)} copy-done((bf16[192,3072]{1,0:T(8,128)(2,1)S(1)}, bf16[192,3072]{1,0:T(8,128)(2,1)}, u32[]{:S(2)}) %copy-start.1) | copy-done | bytes 1179672
  2.6 0.0 copy-start.2
  2.6 1.1 %copy-done.2 = bf16[128,3072]{1,0:T(8,128)(2,1)S(1)} copy-done((bf16[128,3072]{1,0:T(8,128)(2,1)S(1)}, bf16[128,3072]{1,0:T(8,128)(2,1)}, u32[]{:S(2)}) %copy-start.2) | copy-done | bytes 786456
  3.7 0.0 copy-start.3
  3.7 1.1 %copy-done.3 = bf16[128,3072]{1,0:T(8,128)(2,1)S(1)} copy-done((bf16[128,3072]{1,0:T(8,128)(2,1)S(1)}, bf16[128,3072]{1,0:T(8,128)(2,1)}, u32[]{:S(2)}) %copy-start.3) | copy-done | bytes 786456
  4.9 0.0 copy-start.4
  4.9 0.9 %copy-done.4 = f32[16,3072]{1,0:T(8,128)S(1)} copy-done((f32[16,3072]{1,0:T(8,128)S(1)}, f32[16,3072]{1,0:T(8,128)}, u32[]{:S(2)}) %copy-start.4) | copy-done | bytes 196632
  5.8 0.0 copy-start.5
  5.8 0.7 %copy-done.5 = f32[3072]{0:T(1024)S(1)} copy-done((f32[3072]{0:T(1024)S(1)}, f32[3072]{0:T(1024)}, u32[]{:S(2)}) %copy-start.5) | copy-done | bytes 12312
  6.5 0.0 copy-start.6
  6.5 0.7 %copy-done.6 = f32[3072]{0:T(1024)S(1)} copy-done((f32[3072]{0:T(1024)S(1)}, f32[3072]{0:T(1024)}, u32[]{:S(2)}) %copy-start.6) | copy-done | bytes 12312
  7.2 32.4 %shard_map.73 = bf16[128,3072]{1,0:T(8,128)(2,1)S(1)} custom-call(bf16[128,3072]{1,0:T(8,128)(2,1)S(1)} %copy-done.2, bf16[128,3072]{1,0:T(8,128)(2,1)S(1)} %copy-done.3, bf16[224,3072]{1,0:T(8,128)(2,1)S(1)} %bitcast.3, bf16[192,3072]{1,0:T(8,128)(2,1)S(1)} %copy-done.1, f32[1,3072]{1,0:T(1,128)S(1)} %bitcast.4, f32[16,3072]{1,0:T(8,128)S(1)} %copy-done.4, ...), custom_call_target="tpu_custom_call" | custom-call | tf_op jit(solution)/shard_map/pallas_call | solution.py:268
  39.6 0.9 %copy.9 = bf16[128,3072]{1,0:T(8,128)(2,1)} copy(bf16[128,3072]{1,0:T(8,128)(2,1)S(1)} %shard_map.73) | data formatting | bytes 1572864
Async XLA Ops:
  0.0 1.3 %copy-start = (bf16[3072,224]{0,1:T(8,128)(2,1)S(1)}, bf16[3072,224]{0,1:T(8,128)(2,1)}, u32[]{:S(2)}) copy-start(bf16[3072,224]{0,1:T(8,128)(2,1)} %param.9) | copy-start | bytes 4128772
  1.3 1.3 %copy-start.1 = (bf16[192,3072]{1,0:T(8,128)(2,1)S(1)}, bf16[192,3072]{1,0:T(8,128)(2,1)}, u32[]{:S(2)}) copy-start(bf16[192,3072]{1,0:T(8,128)(2,1)} %dtp_hbm.1) | copy-start | bytes 3538948
  2.6 1.1 %copy-start.2 = (bf16[128,3072]{1,0:T(8,128)(2,1)S(1)}, bf16[128,3072]{1,0:T(8,128)(2,1)}, u32[]{:S(2)}) copy-start(bf16[128,3072]{1,0:T(8,128)(2,1)} %u_hbm.1) | copy-start | bytes 2359300
  3.7 1.1 %copy-start.3 = (bf16[128,3072]{1,0:T(8,128)(2,1)S(1)}, bf16[128,3072]{1,0:T(8,128)(2,1)}, u32[]{:S(2)}) copy-start(bf16[128,3072]{1,0:T(8,128)(2,1)} %g_hbm.1) | copy-start | bytes 2359300
  4.9 0.9 %copy-start.4 = (f32[16,3072]{1,0:T(8,128)S(1)}, f32[16,3072]{1,0:T(8,128)}, u32[]{:S(2)}) copy-start(f32[16,3072]{1,0:T(8,128)} %alog_hbm.1) | copy-start | bytes 589828
  5.8 0.7 %copy-start.5 = (f32[3072]{0:T(1024)S(1)}, f32[3072]{0:T(1024)}, u32[]{:S(2)}) copy-start(f32[3072]{0:T(1024)} %param.11) | copy-start | bytes 36868
  6.5 0.7 %copy-start.6 = (f32[3072]{0:T(1024)S(1)}, f32[3072]{0:T(1024)}, u32[]{:S(2)}) copy-start(f32[3072]{0:T(1024)} %param.13) | copy-start | bytes 36868

commit v2 on v1

--- a/solution.py
+++ b/solution.py
@@ -24,7 +24,7 @@
 def kernel(seq, mp, tokens, inner, rank, states,
            u_hbm, g_hbm, xp_hbm, dtp_hbm, bias_hbm, alog_hbm, skip_hbm, out_ref,
            u_ref, g_ref, xp_ref, dtp_ref, bias_ref, alog_ref, skip_ref,
-           proj, bs, cs, rate, raw, dts, drv, ys, tot, sums, got_e, got_s, back, ent, far, near,
+           proj, bs, cs, rate, raw, dts, drv, ys, fades, tot, sums, got_e, got_s, back, ent, far, near,
            in_sem, mp_send, mp_recv, e_send, e_recv, s_send, s_recv, b_send, b_recv,
            f_send, f_recv):
     blocks = pl.cdiv(inner, TILE)
@@ -115,7 +115,10 @@
                 device_id={"seq": base + lax.rem(mine + p, group)},
                 device_id_type=pl.DeviceIdType.MESH).start()
 
-    def scan(k):
+    def cell(t, n):
+        return pl.ds(pl.multiple_of((t * states + n) * SUB, SUB), SUB)
+
+    def ends(k):
         rates = [rate[k, n * SUB:(n + 1) * SUB, :] for n in range(states)]
 
         def body(it, hs):
@@ -124,14 +127,10 @@
                 t = it * UNROLL + i
                 dt = tile(dts, k, t)
                 dr = tile(drv, k, t)
-                acc = [None, None]
                 for n in range(states):
-                    b = bs[n, pl.ds(t, 1), :]
-                    c = cs[n, pl.ds(t, 1), :]
-                    hs[n] = jnp.exp2(rates[n] * dt) * hs[n] + b * dr
-                    term = c * hs[n]
-                    acc[n % 2] = term if acc[n % 2] is None else acc[n % 2] + term
-                ys[k, pl.ds(pl.multiple_of(t * SUB, SUB), SUB), :] = acc[0] + acc[1]
+                    fade = jnp.exp2(rates[n] * dt)
+                    fades[k, cell(t, n), :] = fade
+                    hs[n] = fade * hs[n] + bs[n, pl.ds(t, 1), :] * dr
             return tuple(hs)
 
         zero = jnp.zeros((SUB, LANES), F32)
@@ -148,6 +147,23 @@
                 send_sem=e_send.at[k], recv_sem=e_recv.at[k],
                 device_id={"seq": base + owner},
                 device_id_type=pl.DeviceIdType.MESH).start()
+
+    def local(k):
+        def body(it, hs):
+            hs = list(hs)
+            for i in range(UNROLL):
+                t = it * UNROLL + i
+                dr = tile(drv, k, t)
+                acc = [None, None]
+                for n in range(states):
+                    hs[n] = fades[k, cell(t, n), :] * hs[n] + bs[n, pl.ds(t, 1), :] * dr
+                    term = cs[n, pl.ds(t, 1), :] * hs[n]
+                    acc[n % 2] = term if acc[n % 2] is None else acc[n % 2] + term
+                ys[k, pl.ds(pl.multiple_of(t * SUB, SUB), SUB), :] = acc[0] + acc[1]
+            return tuple(hs)
+
+        zero = jnp.zeros((SUB, LANES), F32)
+        lax.fori_loop(0, tokens // UNROLL, body, (zero,) * states)
 
     def drain(ref, k, sem):
         part = ref.at[k, pl.ds(1, group - 1)]
@@ -195,22 +211,21 @@
 
     def correct(k):
         drain(ent, k, b_recv)
-        rates = [rate[k, n * SUB:(n + 1) * SUB, :] for n in range(states)]
         ents = [ent[k, lax.rem(n - mine + group, group)] for n in range(states)]
 
-        def body(it, total):
+        def body(it, es):
+            es = list(es)
             for i in range(UNROLL):
                 t = it * UNROLL + i
-                total = total + tile(dts, k, t)
                 acc = [tile(ys, k, t), None]
                 for n in range(states):
-                    c = cs[n, pl.ds(t, 1), :]
-                    term = c * (jnp.exp2(rates[n] * total) * ents[n])
+                    es[n] = fades[k, cell(t, n), :] * es[n]
+                    term = cs[n, pl.ds(t, 1), :] * es[n]
                     acc[n % 2] = term if acc[n % 2] is None else acc[n % 2] + term
                 ys[k, pl.ds(pl.multiple_of(t * SUB, SUB), SUB), :] = acc[0] + acc[1]
-            return total
-
-        lax.fori_loop(0, tokens // UNROLL, body, jnp.zeros((SUB, LANES), F32))
+            return tuple(es)
+
+        lax.fori_loop(0, tokens // UNROLL, body, tuple(ents))
 
     def finish(k):
         @pl.loop(0, lanes_of(k))
@@ -229,23 +244,19 @@
         steps(k)
     for n in range(states):
         bs[n] = jnp.broadcast_to(whole[:, rank + n:rank + n + 1], (tokens, LANES))
+    for k in range(blocks):
+        ends(k)
+    for n in range(states):
         cs[n] = jnp.broadcast_to(
             whole[:, rank + states + n:rank + states + n + 1], (tokens, LANES))
     for k in range(blocks):
-        scan(k)
-        if k > 0:
-            own(k - 1)
+        local(k)
+        own(k)
     loads[5].wait()
     loads[6].wait()
-    for k in range(blocks - 1):
+    for k in range(blocks):
         correct(k)
         finish(k)
-        if k == 0:
-            own(blocks - 1)
-    if blocks == 1:
-        own(0)
-    correct(blocks - 1)
-    finish(blocks - 1)
     for k in range(blocks):
         drain(got_s, k, s_send)
         drain(got_e, k, e_send)
@@ -279,6 +290,7 @@
                 pltpu.VMEM((blocks, tokens * SUB, LANES), F32),
                 pltpu.VMEM((blocks, tokens * SUB, LANES), F32),
                 pltpu.VMEM((blocks, tokens * SUB, LANES), F32),
+                pltpu.VMEM((blocks, tokens * states * SUB, LANES), F32),
                 pltpu.VMEM((blocks, states) + cell, F32),
                 pltpu.VMEM((blocks,) + cell, F32),
                 pltpu.VMEM((blocks, group) + cell, F32),
@@ -296,7 +308,7 @@
             ],
             compiler_params=pltpu.CompilerParams(
                 collective_id=0, has_side_effects=True,
-                vmem_limit_bytes=48 * 1024 * 1024),
+                vmem_limit_bytes=62 * 1024 * 1024),
         )(*args)
 
     placed = (

time: 40.9 us -> 32.6 us (0.80)
  local copies, waits for them, and re-layouts: 8.09 us -> 2.06 us
  Pallas kernels: 32.4 us -> 30.4 us
    unnamed x15 -> x1, local copies, waits for them, and re-layouts: 8.09 us -> 2.06 us
    pallas_call x1, Pallas kernels: 32.4 us -> 30.4 us  [per_device(): pl.pallas_call(functools.partial(kernel, seq, mp, tokens, inner, rank, st...]
where the time goes in v2:
time: 32.6 us; the launch traced here: 32.5 us
  Pallas kernels  30.4 us (93%)
  local copies, waits for them, and re-layouts  2.06 us (6%)
    pallas_call x1, Pallas kernels, per_device(): pl.pallas_call(functools.partial(kernel, seq, mp, tokens, inner, rank, st...  30.4 us
    unnamed x1, local copies, waits for them, and re-layouts  2.06 us

profile of v2, /device:TPU:0, one launch (start us, length us, event | category | flops | bytes accessed | tf_op | source)
XLA Modules:
  0.0 32.5 jit_solution(8797345958790801893)
XLA Ops:
  0.0 30.4 %shard_map.73 = bf16[128,3072]{1,0:T(8,128)(2,1)} custom-call(bf16[128,3072]{1,0:T(8,128)(2,1)} %u_hbm.1, bf16[128,3072]{1,0:T(8,128)(2,1)} %g_hbm.1, bf16[224,3072]{1,0:T(8,128)(2,1)} %bitcast.3, bf16[192,3072]{1,0:T(8,128)(2,1)} %dtp_hbm.1, f32[1,3072]{1,0:T(1,128)} %bitcast.4, f32[16,3072]{1,0:T(8,128)} %alog_hbm.1, f32[1,3072]{1,0:T(1,128)} %bitcast.5), custom_call_target="tpu_custom_call" | custom-call | tf_op jit(solution)/shard_map/pallas_call | solution.py:279
  30.4 2.1 %copy.9 = bf16[128,3072]{1,0:T(8,128)(2,1)} copy(bf16[128,3072]{1,0:T(8,128)(2,1)} %shard_map.73) | data formatting | bytes 1572864

commit v3 on v2

--- a/solution.py
+++ b/solution.py
@@ -251,7 +251,10 @@
             whole[:, rank + states + n:rank + states + n + 1], (tokens, LANES))
     for k in range(blocks):
         local(k)
-        own(k)
+        if k < blocks - 1 or blocks == 1:
+            own(k)
+        if k == blocks - 2:
+            own(blocks - 1)
     loads[5].wait()
     loads[6].wait()
     for k in range(blocks):

time: 32.6 us -> 32 us (0.982)
  Pallas kernels: 30.4 us -> 29.8 us
    pallas_call x1, Pallas kernels: 30.4 us -> 29.8 us  [per_device(): pl.pallas_call(functools.partial(kernel, seq, mp, tokens, inner, rank, st...]
where the time goes in v3:
time: 32 us; the launch traced here: 31.8 us
  Pallas kernels  29.8 us (93%)
  local copies, waits for them, and re-layouts  2.06 us (6%)
    pallas_call x1, Pallas kernels, per_device(): pl.pallas_call(functools.partial(kernel, seq, mp, tokens, inner, rank, st...  29.8 us
    unnamed x1, local copies, waits for them, and re-layouts  2.06 us

profile of v3, /device:TPU:0, one launch (start us, length us, event | category | flops | bytes accessed | tf_op | source)
XLA Modules:
  0.0 31.8 jit_solution(10550487113158332042)
XLA Ops:
  0.0 29.8 %shard_map.73 = bf16[128,3072]{1,0:T(8,128)(2,1)} custom-call(bf16[128,3072]{1,0:T(8,128)(2,1)} %u_hbm.1, bf16[128,3072]{1,0:T(8,128)(2,1)} %g_hbm.1, bf16[224,3072]{1,0:T(8,128)(2,1)} %bitcast.3, bf16[192,3072]{1,0:T(8,128)(2,1)} %dtp_hbm.1, f32[1,3072]{1,0:T(1,128)} %bitcast.4, f32[16,3072]{1,0:T(8,128)} %alog_hbm.1, f32[1,3072]{1,0:T(1,128)} %bitcast.5), custom_call_target="tpu_custom_call" | custom-call | tf_op jit(solution)/shard_map/pallas_call | solution.py:282
  29.8 2.1 %copy.9 = bf16[128,3072]{1,0:T(8,128)(2,1)} copy(bf16[128,3072]{1,0:T(8,128)(2,1)} %shard_map.73) | data formatting | bytes 1572864
